TPU v7x, 32 devices: a whole 2x2x4 slice. The times are simulated.
32 devices in a mesh: grp: 8 (over z, y), mem: 4 (over x, core).
Axes of the slice: x: 2, y: 2, z: 4, core: 2. Of those that a mesh axis runs over, the one named last changes fastest.
Arguments:
- codes: bfloat16 [8192, 1024], P(('grp', 'mem')), as said below
- scales: float32 [8192, 8], P(('grp', 'mem')), may hold values from 0.2 to 2
- cluster_id: int32 [8192], P(('grp', 'mem')), may hold values from 0 to 63, as said below
Outputs:
- smoothed: bfloat16 [8192, 1024], P(('grp', 'mem'))
- dup_mass: bfloat16 [8192], P(('grp', 'mem'))
Inputs may be any that keep to these rules, and one draw needn't show every extreme that they name: `cluster_id`: cluster c belongs to owner group c mod 8. Among the 256 documents of one device, at most 40 belong to clusters of any one owner group, and at most 20 to any one cluster; for each index along mem, some owner group gets exactly 40 from every device of that index, and some cluster of that group exactly 20 from every device of that index. `codes`: documents of one cluster lie near a common direction.
All inputs are finite; a program needn't handle non-finite values.
Results may differ from a plain program's by a relative error of at most 0.0034.
Values may be sent and summed in bfloat16 or wider, within the bound.
No kernel may reach another device: no remote copies, remote signals or barrier semaphores. Data moves between devices by JAX's collectives and lax.ppermute only.
A program may use at most 64 MiB of HBM per device.

v0:
```python
import jax
import jax.numpy as jnp
from jax import lax
from jax.sharding import PartitionSpec as P

CAP = 40


def embed(codes, scales):
    rows, width = codes.shape
    nblk = scales.shape[1]
    x = (codes.astype(jnp.float32).reshape(rows, nblk, width // nblk) * scales[:, :, None]).reshape(
        rows, width
    )
    inv = lax.rsqrt(jnp.mean(x * x, axis=1, keepdims=True) + 1e-06)
    return (x * inv).astype(jnp.bfloat16)


def make_fold(queries, qtags, query_index):
    width = queries.shape[1]

    def accumulate(carry, piece, start):
        keys, ktags = piece
        member_count = keys.shape[0]
        sims = (
            lax.dot_general(
                queries, keys, (((1,), (1,)), ((), ())), preferred_element_type=jnp.float32
            )
            / width
        )
        key_index = jnp.arange(member_count, dtype=jnp.int32)
        keep = (
            (qtags[:, None] == ktags[None, :])
            & (qtags[:, None] >= 0)
            & (query_index[:, None] != key_index[None, :])
        )
        weights = jnp.where(keep, jnp.exp(8.0 * (sims - 1.0)), jnp.float32(0.0))
        den_sum = jnp.sum(weights, axis=1)
        numerator_sum = jnp.dot(
            weights.astype(jnp.bfloat16), keys, preferred_element_type=jnp.float32
        )
        return (den_sum, numerator_sum)

    return accumulate


def local(codes, scales, cluster_id):
    rows, width = codes.shape
    groups = lax.axis_size("grp")
    member = lax.axis_index("mem")
    embedding_rows = embed(codes, scales)
    owner = cluster_id % groups
    onehot = (owner[:, None] == jnp.arange(groups, dtype=jnp.int32)[None, :]).astype(jnp.int32)
    ranks = jnp.cumsum(onehot, axis=0) - 1
    slot = jnp.sum(ranks * onehot, axis=1)
    target = owner * CAP + slot
    outbox = (
        jnp.zeros((groups * CAP, width), jnp.bfloat16)
        .at[target]
        .set(embedding_rows)
        .reshape(groups, CAP, width)
    )
    outtags = (
        jnp.full((groups * CAP,), -1.0, jnp.float32)
        .at[target]
        .set(cluster_id.astype(jnp.float32))
        .astype(jnp.bfloat16)
        .reshape(groups, CAP)
    )
    slots = groups * CAP
    inbox, incoming_tags = (
        lax.all_to_all(outbox, "grp", split_axis=0, concat_axis=0, tiled=True),
        lax.all_to_all(outtags, "grp", split_axis=0, concat_axis=0, tiled=True),
    )
    queries = inbox.reshape(slots, width)
    qtags = incoming_tags.reshape(slots)
    start_carry = (jnp.zeros((slots,), jnp.float32), jnp.zeros((slots, width), jnp.float32))
    query_index = member * slots + jnp.arange(slots, dtype=jnp.int32)
    accumulate = make_fold(queries, qtags, query_index)
    den_sum, numerator_sum = accumulate(
        start_carry,
        (
            lax.all_gather(queries, "mem", axis=0, tiled=True),
            lax.all_gather(qtags, "mem", axis=0, tiled=True),
        ),
        jnp.int32(0),
    )
    den = 1.0 + den_sum
    result = ((queries.astype(jnp.float32) + numerator_sum) / den[:, None]).astype(jnp.bfloat16)
    mass = jnp.log(den).astype(jnp.bfloat16)
    back_rows, back_mass = (
        lax.all_to_all(
            result.reshape(groups, CAP, width), "grp", split_axis=0, concat_axis=0, tiled=True
        ),
        lax.all_to_all(mass.reshape(groups, CAP), "grp", split_axis=0, concat_axis=0, tiled=True),
    )
    smoothed = back_rows.reshape(slots, width)[target]
    dup_mass = back_mass.reshape(slots)[target]
    return (smoothed, dup_mass)


def solution(mesh):
    placed = (P(("grp", "mem"), None), P(("grp", "mem"), None), P(("grp", "mem")))
    return jax.shard_map(
        local,
        mesh=mesh,
        in_specs=placed,
        out_specs=(P(("grp", "mem"), None), P(("grp", "mem"))),
        check_vma=False,
    )
```

profile of v0, /device:TPU:0, one launch (start us, length us, event | category | flops | bytes accessed | tf_op | source)
XLA Modules:
  0.0 107.8 jit_solution(3126384838830802530)
XLA Ops:
  7.2 0.0 copy-start.1
  7.2 0.0 all-gather.2.cloned.1.call-start
  7.2 0.8 fusion.14
  8.0 0.6 reduce-window.6
  8.6 0.2 slice_reduce_fusion
  8.8 0.1 fusion.9
  8.9 0.8 copy.7
  9.8 0.3 mul.43
  10.1 0.0 copy-done.1
  10.1 0.3 multiply_reduce_fusion
  10.4 0.0 copy-start.3
  10.4 2.0 %scatter_custom_fusion = bf16[320,1024]{1,0:T(8,128)(2,1)S(1)} fusion(s32[256]{0:T(256)S(1)} %compare_select_fusion, f32[32,8,8,128]{3,2,1,0:T(8,128)S(1)} %bitcast.26, bf16[256,1024]{1,0:T(8,128)(2,1)S(1)} %copy-done.1, f32[256]{0:T(256)S(1)} %add_rsqrt_fusion, bf16[]{:T(256)} %constant.16.clone.1), kind=kCustom, calls=%fused_computation.17 | custom fusion | flops 1048576 | bytes 2229250 | tf_op jit(solution)/shard_map/scatter | solution.py:60
  12.4 24.9 %all_to_all.26 = bf16[8,40,1024]{2,1,0:T(8,128)(2,1)} all-to-all(bf16[8,40,1024]{2,1,0:T(8,128)(2,1)S(1)} %bitcast.30), channel_id=1, replica_groups=mesh['grp'=8,'mem'=4] {'grp'}, dimensions={0} | all-to-all | bytes 1310720 | tf_op jit(solution)/shard_map/all_to_all | solution.py:72
  37.3 0.0 all-gather.2.cloned.1.call-update
  37.3 1.4 %scatter_custom_fusion.1 = f32[320]{0:T(512)S(1)} fusion(s32[256]{0:T(256)S(1)} %compare_select_fusion, f32[256]{0:T(256)S(1)} %get-tuple-element.4, f32[]{:T(128)} %constant.49.clone.1), kind=kCustom, calls=%fused_computation.35 | custom fusion | bytes 1284 | tf_op jit(solution)/shard_map/scatter | solution.py:66
  38.7 0.7 all_to_all.21
  39.4 3.3 %all-to-all-start.1 = ((bf16[8,1,40]{2,1,0:T(2,128)(2,1)}), bf16[8,1,40]{2,1,0:T(2,128)(2,1)S(1)}, u32[]{:S(2)}, u32[]{:S(2)}) async-start(bf16[8,1,40]{2,1,0:T(2,128)(2,1)} %all_to_all.21), calls=%async_computation.1 | async-start | bytes 8192 | tf_op jit(solution)/shard_map/all_to_all | solution.py:73
  42.8 0.0 copy-done.3
  42.8 0.6 dynamic-slice
  44.0 5.1 %all-to-all-done.1 = bf16[8,1,40]{2,1,0:T(2,128)(2,1)S(1)} async-done(((bf16[8,1,40]{2,1,0:T(2,128)(2,1)}), bf16[8,1,40]{2,1,0:T(2,128)(2,1)S(1)}, u32[]{:S(2)}, u32[]{:S(2)}) %all-to-all-start.1) | async-done | bytes 672 | tf_op jit(solution)/shard_map/all_to_all | solution.py:73
  49.1 0.1 reshape.140
  49.2 0.3 dynamic-update-slice
  49.4 6.1 %all-reduce = bf16[1280]{0:T(1024)(128)(2,1)S(1)} all-reduce(bf16[1280]{0:T(1024)(128)(2,1)S(1)} %dynamic-update-slice), channel_id=1, replica_groups=mesh['grp'=8,'mem'=4] {'mem'}, use_global_device_ids=true, to_apply=%add | all-reduce | flops 1280 | bytes 5120
  55.6 0.0 copy-start
  55.6 6.2 %all-gather.2.cloned.1.call-done = bf16[1280,1024]{1,0:T(8,128)(2,1)} async-done(((bf16[320,1024]{1,0:T(8,128)(2,1)}), bf16[1280,1024]{1,0:T(8,128)(2,1)}) %all-gather.2.cloned.1.call-update) | async-done | bytes 2621456 | tf_op jit(solution)/shard_map/all_gather | solution.py:83
  61.8 0.0 copy-start.2
  61.8 4.5 %fusion.15 = (f32[320]{0:T(512)S(1)}, bf16[320,1280]{1,0:T(8,128)(2,1)}) fusion(bf16[320,1024]{1,0:T(8,128)(2,1)} %bitcast.28, bf16[1280,1024]{1,0:T(8,128)(2,1)} %all-gather.2.cloned.1.call-done, s32[320]{0:T(512)S(1)} %iota_add_fusion, pred[320]{0:T(512)(128)(4,1)S(1)} %broadcast_compare_fusion, bf16[1280]{0:T(1024)(128)(2,1)S(1)} %all-reduce, ...), kind=kOutput, calls=%fused_computation.40 | convolution fusion | flops 843775680 | bytes 4102080 | tf_op jit(solution)/shard_map/dot_general | solution.py:26
  66.3 0.7 convert_element_type.50
  67.0 5.5 %all-to-all-start.3 = ((bf16[8,1,40]{2,1,0:T(2,128)(2,1)}), bf16[8,1,40]{2,1,0:T(2,128)(2,1)S(1)}, u32[]{:S(2)}, u32[]{:S(2)}) async-start(bf16[8,1,40]{2,1,0:T(2,128)(2,1)} %convert_element_type.50), calls=%async_computation.3 | async-start | bytes 8192 | tf_op jit(solution)/shard_map/all_to_all | solution.py:95
  72.5 0.0 copy-done
  72.5 0.0 copy-done.2
  72.5 3.1 %divide_convert_fusion = bf16[320,1024]{1,0:T(8,128)(2,1)} fusion(bf16[1280,1024]{1,0:T(8,128)(2,1)S(1)} %copy-done.2, bf16[320,1024]{1,0:T(8,128)(2,1)S(1)} %bitcast.29, bf16[320,1280]{1,0:T(8,128)(2,1)} %get-tuple-element.7, f32[320]{0:T(512)S(1)} %get-tuple-element.3), kind=kOutput, calls=%fused_computation.12 | convolution fusion | flops 840171520 | bytes 4752640 | tf_op jit(solution)/shard_map/dot_general | solution.py:39
  75.6 3.3 %all-to-all-done.3 = bf16[8,1,40]{2,1,0:T(2,128)(2,1)S(1)} async-done(((bf16[8,1,40]{2,1,0:T(2,128)(2,1)}), bf16[8,1,40]{2,1,0:T(2,128)(2,1)S(1)}, u32[]{:S(2)}, u32[]{:S(2)}) %all-to-all-start.3) | async-done | bytes 672 | tf_op jit(solution)/shard_map/all_to_all | solution.py:95
  78.9 3.5 %all-to-all-start.2 = ((bf16[8,40,1024]{2,1,0:T(8,128)(2,1)}), bf16[8,40,1024]{2,1,0:T(8,128)(2,1)S(1)}, u32[]{:S(2)}, u32[]{:S(2)}) async-start(bf16[8,40,1024]{2,1,0:T(8,128)(2,1)} %bitcast.6), calls=%async_computation.2 | async-start | bytes 1310720 | tf_op jit(solution)/shard_map/all_to_all | solution.py:92
  82.5 0.1 reshape.103
  82.6 2.5 %gather_fusion.1 = bf16[256]{0:T(256)(128)(2,1)} fusion(bf16[320]{0:T(512)(128)(2,1)S(1)} %reshape.103, s32[1024]{0:T(1024)S(1)} %pad_clamp_fusion), kind=kCustom, calls=%fused_computation.1 | custom fusion | bytes 2048 | tf_op jit(solution)/shard_map/gather | solution.py:98
  85.0 13.9 %all-to-all-done.2 = bf16[8,40,1024]{2,1,0:T(8,128)(2,1)S(1)} async-done(((bf16[8,40,1024]{2,1,0:T(8,128)(2,1)}), bf16[8,40,1024]{2,1,0:T(8,128)(2,1)S(1)}, u32[]{:S(2)}, u32[]{:S(2)}) %all-to-all-start.2) | async-done | bytes 655392 | tf_op jit(solution)/shard_map/all_to_all | solution.py:92
  98.9 2.0 %gather_fusion = bf16[256,1024]{1,0:T(8,128)(2,1)} fusion(bf16[320,1024]{1,0:T(8,128)(2,1)S(1)} %bitcast.24, s32[1024]{0:T(1024)S(1)} %pad_clamp_fusion), kind=kCustom, calls=%fused_computation | custom fusion | bytes 1049600 | tf_op jit(solution)/shard_map/gather | solution.py:97
  (13 shorter events, 0.1 us)
Async XLA Ops:
  7.2 2.9 %copy-start.1 = (bf16[256,1024]{1,0:T(8,128)(2,1)S(1)}, bf16[256,1024]{1,0:T(8,128)(2,1)}, u32[]{:S(2)}) copy-start(bf16[256,1024]{1,0:T(8,128)(2,1)} %param.3) | copy-start | bytes 1572868
  7.2 54.6 %all-gather.2.cloned.1.call-start = ((), (), s32[]{:S(2)}) async-start(), calls=%async_computation.4 | async-start | bytes 3276800 | tf_op jit(solution)/shard_map/all_gather | solution.py:83
  10.4 32.4 %copy-start.3 = (u32[32]{0:T(128)S(1)}, u32[32]{0:T(128)}, u32[]{:S(2)}) copy-start(u32[32]{0:T(128)} %constant.55) | copy-start | bytes 388
  39.4 9.6 %all-to-all-start.1 = ((bf16[8,1,40]{2,1,0:T(2,128)(2,1)}), bf16[8,1,40]{2,1,0:T(2,128)(2,1)S(1)}, u32[]{:S(2)}, u32[]{:S(2)}) async-start(bf16[8,1,40]{2,1,0:T(2,128)(2,1)} %all_to_all.21), calls=%async_computation.1 | async-start | bytes 8192 | tf_op jit(solution)/shard_map/all_to_all | solution.py:73
  55.6 16.9 %copy-start = (bf16[8,40,1024]{2,1,0:T(8,128)(2,1)S(1)}, bf16[8,40,1024]{2,1,0:T(8,128)(2,1)}, u32[]{:S(2)}) copy-start(bf16[8,40,1024]{2,1,0:T(8,128)(2,1)} %all_to_all.26) | copy-start | bytes 1966084
  61.8 10.7 %copy-start.2 = (bf16[1280,1024]{1,0:T(8,128)(2,1)S(1)}, bf16[1280,1024]{1,0:T(8,128)(2,1)}, u32[]{:S(2)}) copy-start(bf16[1280,1024]{1,0:T(8,128)(2,1)} %all-gather.2.cloned.1.call-done) | copy-start | bytes 7864324
  67.0 11.9 %all-to-all-start.3 = ((bf16[8,1,40]{2,1,0:T(2,128)(2,1)}), bf16[8,1,40]{2,1,0:T(2,128)(2,1)S(1)}, u32[]{:S(2)}, u32[]{:S(2)}) async-start(bf16[8,1,40]{2,1,0:T(2,128)(2,1)} %convert_element_type.50), calls=%async_computation.3 | async-start | bytes 8192 | tf_op jit(solution)/shard_map/all_to_all | solution.py:95
  78.9 20.1 %all-to-all-start.2 = ((bf16[8,40,1024]{2,1,0:T(8,128)(2,1)}), bf16[8,40,1024]{2,1,0:T(8,128)(2,1)S(1)}, u32[]{:S(2)}, u32[]{:S(2)}) async-start(bf16[8,40,1024]{2,1,0:T(8,128)(2,1)} %bitcast.6), calls=%async_computation.2 | async-start | bytes 1310720 | tf_op jit(solution)/shard_map/all_to_all | solution.py:92
Sparse Core Ops, SparseCore 0:
  37.4 24.3 all-gather.1
where the time goes:
time: 108 us
  blocking collectives  31 us (29%)
  waiting for transfers between devices  28.5 us (26%)
  between operations  14.8 us (14%)
  starting transfers between devices  12.4 us (11%)
  local copies, waits for them, and re-layouts  9.58 us (9%)
  matrix products  7.54 us (7%)
  other arithmetic  3.82 us (4%)
    all_to_all x1, blocking collectives, local(): lax.all_to_all(outbox, 'grp', split_axis=0, concat_axis=0, tiled=True)  24.9 us
    all_to_all x1, waiting for transfers between devices, local(): lax.all_to_all(result.reshape(groups, CAP, width), 'grp', split_axis=0, c...  13.9 us
    all_gather x1, waiting for transfers between devices, local(): lax.all_gather(queries, 'mem', axis=0, tiled=True)  6.2 us
    unnamed x1, blocking collectives  6.14 us
    all_to_all x1, starting transfers between devices, local(): lax.all_to_all(mass.reshape(groups, CAP), 'grp', split_axis=0, concat_axi...  5.52 us
    all_to_all x1, waiting for transfers between devices, local(): lax.all_to_all(outtags, 'grp', split_axis=0, concat_axis=0, tiled=True)  5.05 us
    dot_general x1, matrix products, accumulate(): lax.dot_general(queries, keys, (((1,), (1,)), ((), ())), preferred_elemen...  4.49 us
    all_to_all x1, starting transfers between devices, local(): lax.all_to_all(result.reshape(groups, CAP, width), 'grp', split_axis=0, c...  3.54 us
  transfers between devices with their start and end apart: 4, of which 4 were waited for; matrix products, arithmetic and copies ran while one was open for 7% of the time, Pallas kernels for 0%

commit v1 on v0

--- a/solution.py
+++ b/solution.py
@@ -4,6 +4,12 @@
 from jax.sharding import PartitionSpec as P
 
 CAP = 40
+
+
+def tiled_gather(x, axis, dim):
+    count = lax.axis_size(axis)
+    repeats = [count if d == dim else 1 for d in range(x.ndim)]
+    return lax.all_to_all(jnp.tile(x, repeats), axis, split_axis=dim, concat_axis=dim, tiled=True)
 
 
 def embed(codes, scales):
@@ -79,10 +85,7 @@
     accumulate = make_fold(queries, qtags, query_index)
     den_sum, numerator_sum = accumulate(
         start_carry,
-        (
-            lax.all_gather(queries, "mem", axis=0, tiled=True),
-            lax.all_gather(qtags, "mem", axis=0, tiled=True),
-        ),
+        (tiled_gather(queries, "mem", 0), lax.all_gather(qtags, "mem", axis=0, tiled=True)),
         jnp.int32(0),
     )
     den = 1.0 + den_sum

time: 108 us -> 111 us (1.028)
  blocking collectives: 31 us -> 51.1 us
  between operations: 14.8 us -> 1.43 us
  waiting for transfers between devices: 28.5 us -> 19.7 us
  starting transfers between devices: 12.4 us -> 17.9 us
  matrix products: 7.54 us -> 5.48 us
  local copies, waits for them, and re-layouts: 9.58 us -> 11.4 us
    unnamed x1, blocking collectives: 6.14 us -> 31.1 us
    all_gather x1 -> x0, waiting for transfers between devices: 6.2 us -> none  [local(): lax.all_gather(queries, 'mem', axis=0, tiled=True)]
    all_to_all x1, blocking collectives: 24.9 us -> 20 us  [local(): lax.all_to_all(outbox, 'grp', split_axis=0, concat_axis=0, tiled=True)]
    all_to_all x1, starting transfers between devices: 3.31 us -> 7.28 us  [local(): lax.all_to_all(outtags, 'grp', split_axis=0, concat_axis=0, tiled=True)]
    all_to_all x0 -> x1, starting transfers between devices: none -> 3.78 us  [tiled_gather(): lax.all_to_all(jnp.tile(x, repeats), axis, split_axis=dim, concat_axis=di...]
    all_to_all x1, starting transfers between devices: 5.52 us -> 3.31 us  [local(): lax.all_to_all(mass.reshape(groups, CAP), 'grp', split_axis=0, concat_axi...]
    all_to_all x1, waiting for transfers between devices: 5.05 us -> 2.95 us  [local(): lax.all_to_all(outtags, 'grp', split_axis=0, concat_axis=0, tiled=True)]
    dot_general x1, matrix products: 4.49 us -> 2.43 us  [accumulate(): lax.dot_general(queries, keys, (((1,), (1,)), ((), ())), preferred_elemen...]
  transfers between devices with their start and end apart: 4 -> 4, of which waited for: 4 -> 3; matrix products, arithmetic and copies ran while one was open for 7% -> 9% of each run, Pallas kernels for 0% -> 0%
where the time goes in v1:
time: 111 us
  blocking collectives  51.1 us (46%)
  waiting for transfers between devices  19.7 us (18%)
  starting transfers between devices  17.9 us (16%)
  local copies, waits for them, and re-layouts  11.4 us (10%)
  matrix products  5.48 us (5%)
  other arithmetic  3.83 us (3%)
  between operations  1.43 us (1%)
    unnamed x1, blocking collectives  31.1 us
    all_to_all x1, blocking collectives, local(): lax.all_to_all(outbox, 'grp', split_axis=0, concat_axis=0, tiled=True)  20 us
    all_to_all x1, waiting for transfers between devices, local(): lax.all_to_all(result.reshape(groups, CAP, width), 'grp', split_axis=0, c...  13.5 us
    all_to_all x1, starting transfers between devices, local(): lax.all_to_all(outtags, 'grp', split_axis=0, concat_axis=0, tiled=True)  7.28 us
    all_to_all x1, starting transfers between devices, tiled_gather(): lax.all_to_all(jnp.tile(x, repeats), axis, split_axis=dim, concat_axis=di...  3.78 us
    all_to_all x1, starting transfers between devices, local(): lax.all_to_all(result.reshape(groups, CAP, width), 'grp', split_axis=0, c...  3.54 us
    all_to_all x1, starting transfers between devices, local(): lax.all_to_all(mass.reshape(groups, CAP), 'grp', split_axis=0, concat_axi...  3.31 us
    all_to_all x1, waiting for transfers between devices, local(): lax.all_to_all(mass.reshape(groups, CAP), 'grp', split_axis=0, concat_axi...  3.28 us
  transfers between devices with their start and end apart: 4, of which 3 were waited for; matrix products, arithmetic and copies ran while one was open for 9% of the time, Pallas kernels for 0%

profile of v1, /device:TPU:0, one launch (start us, length us, event | category | flops | bytes accessed | tf_op | source)
XLA Modules:
  0.0 110.9 jit_solution(17379971462033012531)
XLA Ops:
  0.6 0.0 copy-start
  0.6 0.8 fusion.14
  1.4 0.6 reduce-window.6
  2.0 0.2 slice_reduce_fusion
  2.2 0.1 fusion.9
  2.4 1.4 %scatter_custom_fusion.1 = f32[320]{0:T(512)S(1)} fusion(s32[256]{0:T(256)S(1)} %compare_select_fusion, f32[256]{0:T(256)S(1)} %get-tuple-element.4, f32[]{:T(128)} %constant.49.clone.1), kind=kCustom, calls=%fused_computation.35 | custom fusion | bytes 1284 | tf_op jit(solution)/shard_map/scatter | solution.py:72
  3.8 0.7 all_to_all.29
  4.5 7.3 %all-to-all-start.1 = ((bf16[8,1,40]{2,1,0:T(2,128)(2,1)}), bf16[8,1,40]{2,1,0:T(2,128)(2,1)S(1)}, u32[]{:S(2)}, u32[]{:S(2)}) async-start(bf16[8,1,40]{2,1,0:T(2,128)(2,1)} %all_to_all.29), calls=%async_computation.1 | async-start | bytes 8192 | tf_op jit(solution)/shard_map/all_to_all | solution.py:79
  11.7 0.8 copy.7
  12.6 0.3 mul.43
  12.9 0.0 copy-done
  12.9 0.3 multiply_reduce_fusion
  13.2 2.0 %scatter_custom_fusion = bf16[320,1024]{1,0:T(8,128)(2,1)S(1)} fusion(s32[256]{0:T(256)S(1)} %compare_select_fusion, f32[32,8,8,128]{3,2,1,0:T(8,128)S(1)} %bitcast.27, bf16[256,1024]{1,0:T(8,128)(2,1)S(1)} %copy-done, f32[256]{0:T(256)S(1)} %add_rsqrt_fusion, bf16[]{:T(256)} %constant.16.clone.1), kind=kCustom, calls=%fused_computation.17 | custom fusion | flops 1048576 | bytes 2229250 | tf_op jit(solution)/shard_map/scatter | solution.py:66
  15.2 2.9 %all-to-all-done.1 = bf16[8,1,40]{2,1,0:T(2,128)(2,1)S(1)} async-done(((bf16[8,1,40]{2,1,0:T(2,128)(2,1)}), bf16[8,1,40]{2,1,0:T(2,128)(2,1)S(1)}, u32[]{:S(2)}, u32[]{:S(2)}) %all-to-all-start.1) | async-done | bytes 672 | tf_op jit(solution)/shard_map/all_to_all | solution.py:79
  18.1 20.0 %all_to_all.35 = bf16[8,40,1024]{2,1,0:T(8,128)(2,1)S(1)} all-to-all(bf16[8,40,1024]{2,1,0:T(8,128)(2,1)S(1)} %bitcast.33), channel_id=1, replica_groups=mesh['grp'=8,'mem'=4] {'grp'}, dimensions={0} | all-to-all | bytes 1310720 | tf_op jit(solution)/shard_map/all_to_all | solution.py:78
  38.1 1.8 %tile.2 = bf16[4,320,1024]{2,1,0:T(8,128)(2,1)} broadcast(bf16[320,1024]{1,0:T(8,128)(2,1)S(1)} %bitcast.30), dimensions={1,2} | broadcast | bytes 3276800 | tf_op jit(solution)/shard_map/tile | solution.py:12
  40.0 0.0 copy-start.1
  40.0 3.8 %all-to-all-start.2 = ((bf16[4,320,1024]{2,1,0:T(8,128)(2,1)}), bf16[4,320,1024]{2,1,0:T(8,128)(2,1)S(1)}, u32[]{:S(2)}, u32[]{:S(2)}) async-start(bf16[4,320,1024]{2,1,0:T(8,128)(2,1)} %tile.2), calls=%async_computation.2 | async-start | bytes 5242880 | tf_op jit(solution)/shard_map/all_to_all | solution.py:12
  43.8 0.0 copy-done.1
  43.8 0.6 dynamic-slice
  45.1 0.1 reshape.147
  45.2 0.3 dynamic-update-slice
  45.4 31.1 %all-reduce = bf16[1280]{0:T(1024)(128)(2,1)S(1)} all-reduce(bf16[1280]{0:T(1024)(128)(2,1)S(1)} %dynamic-update-slice), channel_id=1, replica_groups=mesh['grp'=8,'mem'=4] {'mem'}, use_global_device_ids=true, to_apply=%add | all-reduce | flops 1280 | bytes 5120
  76.5 0.0 all-to-all-done.2
  76.5 2.4 %fusion.15 = (f32[320]{0:T(512)S(1)}, bf16[320,1280]{1,0:T(8,128)(2,1)}) fusion(bf16[320,1024]{1,0:T(8,128)(2,1)S(1)} %bitcast.31, bf16[1280,1024]{1,0:T(8,128)(2,1)S(1)} %bitcast.28, s32[320]{0:T(512)S(1)} %iota_add_fusion, pred[320]{0:T(512)(128)(4,1)S(1)} %broadcast_compare_fusion, bf16[1280]{0:T(1024)(128)(2,1)S(1)} %all-reduce, ...), kind=kOutput, calls=%fused_computation.40 | convolution fusion | flops 843775680 | bytes 4102080 | tf_op jit(solution)/shard_map/dot_general | solution.py:32
  79.0 0.7 convert_element_type.50
  79.6 3.3 %all-to-all-start.4 = ((bf16[8,1,40]{2,1,0:T(2,128)(2,1)}), bf16[8,1,40]{2,1,0:T(2,128)(2,1)S(1)}, u32[]{:S(2)}, u32[]{:S(2)}) async-start(bf16[8,1,40]{2,1,0:T(2,128)(2,1)} %convert_element_type.50), calls=%async_computation.4 | async-start | bytes 8192 | tf_op jit(solution)/shard_map/all_to_all | solution.py:98
  83.0 3.0 %divide_convert_fusion = bf16[320,1024]{1,0:T(8,128)(2,1)} fusion(bf16[1280,1024]{1,0:T(8,128)(2,1)S(1)} %bitcast.29, bf16[320,1024]{1,0:T(8,128)(2,1)S(1)} %bitcast.32, bf16[320,1280]{1,0:T(8,128)(2,1)} %get-tuple-element.7, f32[320]{0:T(512)S(1)} %get-tuple-element.3), kind=kOutput, calls=%fused_computation.12 | convolution fusion | flops 840171520 | bytes 4752640 | tf_op jit(solution)/shard_map/dot_general | solution.py:45
  86.0 3.3 %all-to-all-done.4 = bf16[8,1,40]{2,1,0:T(2,128)(2,1)S(1)} async-done(((bf16[8,1,40]{2,1,0:T(2,128)(2,1)}), bf16[8,1,40]{2,1,0:T(2,128)(2,1)S(1)}, u32[]{:S(2)}, u32[]{:S(2)}) %all-to-all-start.4) | async-done | bytes 672 | tf_op jit(solution)/shard_map/all_to_all | solution.py:98
  89.3 3.5 %all-to-all-start.3 = ((bf16[8,40,1024]{2,1,0:T(8,128)(2,1)}), bf16[8,40,1024]{2,1,0:T(8,128)(2,1)S(1)}, u32[]{:S(2)}, u32[]{:S(2)}) async-start(bf16[8,40,1024]{2,1,0:T(8,128)(2,1)} %bitcast.34), calls=%async_computation.3 | async-start | bytes 1310720 | tf_op jit(solution)/shard_map/all_to_all | solution.py:95
  92.9 0.1 reshape.110
  93.0 2.5 %gather_fusion.1 = bf16[256]{0:T(256)(128)(2,1)} fusion(bf16[320]{0:T(512)(128)(2,1)S(1)} %reshape.110, s32[1024]{0:T(1024)S(1)} %pad_clamp_fusion), kind=kCustom, calls=%fused_computation.1 | custom fusion | bytes 2048 | tf_op jit(solution)/shard_map/gather | solution.py:101
  95.4 13.5 %all-to-all-done.3 = bf16[8,40,1024]{2,1,0:T(8,128)(2,1)S(1)} async-done(((bf16[8,40,1024]{2,1,0:T(8,128)(2,1)}), bf16[8,40,1024]{2,1,0:T(8,128)(2,1)S(1)}, u32[]{:S(2)}, u32[]{:S(2)}) %all-to-all-start.3) | async-done | bytes 655392 | tf_op jit(solution)/shard_map/all_to_all | solution.py:95
  108.9 2.0 %gather_fusion = bf16[256,1024]{1,0:T(8,128)(2,1)} fusion(bf16[320,1024]{1,0:T(8,128)(2,1)S(1)} %bitcast.25, s32[1024]{0:T(1024)S(1)} %pad_clamp_fusion), kind=kCustom, calls=%fused_computation | custom fusion | bytes 1049600 | tf_op jit(solution)/shard_map/gather | solution.py:100
  (13 shorter events, 0.1 us)
Async XLA Ops:
  0.6 12.3 %copy-start = (bf16[256,1024]{1,0:T(8,128)(2,1)S(1)}, bf16[256,1024]{1,0:T(8,128)(2,1)}, u32[]{:S(2)}) copy-start(bf16[256,1024]{1,0:T(8,128)(2,1)} %param.3) | copy-start | bytes 1572868
  4.5 13.7 %all-to-all-start.1 = ((bf16[8,1,40]{2,1,0:T(2,128)(2,1)}), bf16[8,1,40]{2,1,0:T(2,128)(2,1)S(1)}, u32[]{:S(2)}, u32[]{:S(2)}) async-start(bf16[8,1,40]{2,1,0:T(2,128)(2,1)} %all_to_all.29), calls=%async_computation.1 | async-start | bytes 8192 | tf_op jit(solution)/shard_map/all_to_all | solution.py:79
  40.0 3.8 %copy-start.1 = (u32[32]{0:T(128)S(1)}, u32[32]{0:T(128)}, u32[]{:S(2)}) copy-start(u32[32]{0:T(128)} %constant.55) | copy-start | bytes 388
  40.0 36.5 %all-to-all-start.2 = ((bf16[4,320,1024]{2,1,0:T(8,128)(2,1)}), bf16[4,320,1024]{2,1,0:T(8,128)(2,1)S(1)}, u32[]{:S(2)}, u32[]{:S(2)}) async-start(bf16[4,320,1024]{2,1,0:T(8,128)(2,1)} %tile.2), calls=%async_computation.2 | async-start | bytes 5242880 | tf_op jit(solution)/shard_map/all_to_all | solution.py:12
  79.6 9.6 %all-to-all-start.4 = ((bf16[8,1,40]{2,1,0:T(2,128)(2,1)}), bf16[8,1,40]{2,1,0:T(2,128)(2,1)S(1)}, u32[]{:S(2)}, u32[]{:S(2)}) async-start(bf16[8,1,40]{2,1,0:T(2,128)(2,1)} %convert_element_type.50), calls=%async_computation.4 | async-start | bytes 8192 | tf_op jit(solution)/shard_map/all_to_all | solution.py:98
  89.3 19.6 %all-to-all-start.3 = ((bf16[8,40,1024]{2,1,0:T(8,128)(2,1)}), bf16[8,40,1024]{2,1,0:T(8,128)(2,1)S(1)}, u32[]{:S(2)}, u32[]{:S(2)}) async-start(bf16[8,40,1024]{2,1,0:T(8,128)(2,1)} %bitcast.34), calls=%async_computation.3 | async-start | bytes 1310720 | tf_op jit(solution)/shard_map/all_to_all | solution.py:95
